TPU v7x, 32 devices: a whole 2x2x4 slice. The times are simulated.
32 devices in a mesh: expert: 8 (over y, x, core), dp: 4 (over z).
Axes of the slice: x: 2, y: 2, z: 4, core: 2. Of those that a mesh axis runs over, the one named last changes fastest.
Arguments:
- tokens: bfloat16 [4096, 2048], P(('expert', 'dp')), may hold values from -6 to 6
- out_grad: bfloat16 [4096, 2048], P(('expert', 'dp')), may hold values from -1.25 to 1.25
- expert_ids: int32 [4096, 8], P(('expert', 'dp')), may hold values from 0 to 15, all different within a row; in each aligned block of 128 rows (0 to 127, 128 to 255, ...) at most 72 rows name the same one
- route_weight: bfloat16 [4096, 8], P(('expert', 'dp')), may hold values from 0.099609375 to 1
- w_gate_up: bfloat16 [16, 2048, 768], P('expert'), may hold values from -0.125 to 0.125
- w_down: bfloat16 [16, 384, 2048], P('expert'), may hold values from -0.3125 to 0.3125
Outputs:
- d_tokens: bfloat16 [4096, 2048], P(('expert', 'dp'))
- d_route: bfloat16 [4096, 8], P(('expert', 'dp'))
- grad_gate_up: bfloat16 [16, 2048, 768], P('expert', 'dp')
- grad_down: bfloat16 [16, 384, 2048], P('expert', None, 'dp')
Inputs may be any that keep to these rules, and one draw needn't show every extreme that they name: `expert_ids`: each row names 8 different experts. Among the 128 rows of one device (aligned blocks of 128 rows) no expert is named more than 72 times, and in every draw some expert is named exactly 72 times by the rows of some device.
All inputs are finite; a program needn't handle non-finite values.
Results may differ from a plain program's by a relative error of at most 0.012.
Values may be sent and summed in bfloat16 or wider, within the bound.
A program may use at most 128 MiB of HBM per device.

v0:
```python
import jax
import jax.numpy as jnp
from jax import lax
from jax.sharding import PartitionSpec as P


def expert_backward(rows_in, rows_grad, weight, gate_up, down):
    pre_act = jnp.dot(rows_in, gate_up, preferred_element_type=jnp.float32)
    half_width = pre_act.shape[1] // 2
    gate_pre = pre_act[:, :half_width]
    up_pre = pre_act[:, half_width:]
    sigmoid_gate = jax.nn.sigmoid(gate_pre)
    active = gate_pre * sigmoid_gate
    hidden = (active * up_pre).astype(jnp.bfloat16)
    back_hidden = lax.dot_general(
        rows_grad, down, (((1,), (1,)), ((), ())), preferred_element_type=jnp.float32
    )
    route_grad = jnp.sum(back_hidden * hidden.astype(jnp.float32), axis=1).astype(jnp.bfloat16)
    weight_col = weight.astype(jnp.float32)[:, None]
    scaled = weight_col * back_hidden
    grad_gate = scaled * up_pre * sigmoid_gate * (1.0 + gate_pre * (1.0 - sigmoid_gate))
    grad_up = scaled * active
    grad_pre = jnp.concatenate([grad_gate, grad_up], axis=1).astype(jnp.bfloat16)
    route_input = lax.dot_general(
        grad_pre, gate_up, (((1,), (1,)), ((), ())), preferred_element_type=jnp.float32
    ).astype(jnp.bfloat16)
    scaled_hidden = (weight_col * hidden.astype(jnp.float32)).astype(jnp.bfloat16)
    return (route_input, route_grad, grad_pre, scaled_hidden)


def weight_terms(rows_in, rows_grad, grad_pre, scaled_hidden):
    term_gate_up = lax.dot_general(
        rows_in, grad_pre, (((0,), (0,)), ((), ())), preferred_element_type=jnp.float32
    )
    term_down = lax.dot_general(
        scaled_hidden, rows_grad, (((0,), (0,)), ((), ())), preferred_element_type=jnp.float32
    )
    return (term_gate_up, term_down)


def run_expert(arrived_in, arrived_grad, arrived_weight, gate_up, down):
    groups = arrived_in.shape[0]
    capacity = arrived_in.shape[1]
    dim_model = arrived_in.shape[2]
    rows_in = arrived_in.reshape(groups * capacity, dim_model)
    rows_grad = arrived_grad.reshape(groups * capacity, dim_model)
    weight = arrived_weight.reshape(groups * capacity)
    route_input, route_grad, grad_pre, scaled_hidden = expert_backward(
        rows_in, rows_grad, weight, gate_up, down
    )
    shaped_input = route_input.reshape(groups, capacity, dim_model)
    shaped_grad = route_grad.reshape(groups, capacity)
    return (shaped_input, shaped_grad, (rows_in, rows_grad, grad_pre, scaled_hidden))


def slot_numbers(route_experts, all_experts):
    route_count = route_experts.shape[0]
    block_len = 128
    block_count = route_count // block_len
    onehot = (route_experts[:, None] == jnp.arange(all_experts, dtype=jnp.int32)[None, :]).astype(
        jnp.bfloat16
    )
    onehot = onehot.reshape(block_count, block_len, all_experts)
    lower = (jnp.arange(block_len)[:, None] > jnp.arange(block_len)[None, :]).astype(jnp.bfloat16)
    within = jnp.einsum("ij,bje->bie", lower, onehot, preferred_element_type=jnp.float32)
    totals = jnp.sum(onehot.astype(jnp.float32), axis=1)
    earlier = (jnp.arange(block_count)[:, None] > jnp.arange(block_count)[None, :]).astype(
        jnp.float32
    )
    before = jnp.dot(earlier, totals, precision=lax.Precision.HIGHEST)
    counted = jnp.sum((within + before[:, None, :]) * onehot.astype(jnp.float32), axis=2)
    return counted.reshape(route_count).astype(jnp.int32)


def local(tokens, out_grad, expert_ids, route_weight, w_gate_up, w_down):
    tok_rows = tokens.shape[0]
    dim_model = tokens.shape[1]
    top_count = expert_ids.shape[1]
    exp_local = w_gate_up.shape[0]
    groups = lax.axis_size("expert")
    all_experts = exp_local * groups
    route_count = tok_rows * top_count
    capacity = 9 * tok_rows * top_count // (8 * all_experts)
    route_experts = expert_ids.reshape(route_count)
    slot_index = slot_numbers(route_experts, all_experts)
    target = route_experts // exp_local
    local_expert = route_experts % exp_local
    position = local_expert * (groups * capacity) + target * capacity + slot_index
    source_table = jnp.full((all_experts * capacity,), route_count, jnp.int32)
    source_table = source_table.at[position].set(jnp.arange(route_count, dtype=jnp.int32))
    token_of = source_table // top_count
    send_in = jnp.take(tokens, token_of, axis=0, mode="fill", fill_value=0).reshape(
        exp_local, groups, capacity, dim_model
    )
    send_grad = jnp.take(out_grad, token_of, axis=0, mode="fill", fill_value=0).reshape(
        exp_local, groups, capacity, dim_model
    )
    send_weight = jnp.take(
        route_weight.reshape(route_count), source_table, axis=0, mode="fill", fill_value=0
    ).reshape(exp_local, groups, capacity)
    gate_up_terms = []
    down_terms = []
    arrived_in, arrived_grad, arrived_weight = (
        lax.all_to_all(send_in, "expert", split_axis=1, concat_axis=1, tiled=True),
        lax.all_to_all(send_grad, "expert", split_axis=1, concat_axis=1, tiled=True),
        lax.all_to_all(send_weight, "expert", split_axis=1, concat_axis=1, tiled=True),
    )
    inputs_list = []
    grads_list = []
    saved = []
    for which in range(exp_local):
        shaped_input, shaped_grad, kept = run_expert(
            arrived_in[which],
            arrived_grad[which],
            arrived_weight[which],
            w_gate_up[which],
            w_down[which],
        )
        inputs_list.append(shaped_input)
        grads_list.append(shaped_grad)
        saved.append(kept)
    returned_in, returned_route = (
        lax.all_to_all(jnp.stack(inputs_list), "expert", split_axis=1, concat_axis=1, tiled=True),
        lax.all_to_all(jnp.stack(grads_list), "expert", split_axis=1, concat_axis=1, tiled=True),
    )
    for which in range(exp_local):
        term_gate_up, term_down = weight_terms(*saved[which])
        gate_up_terms.append(term_gate_up)
        down_terms.append(term_down)
    summed_gate_up, summed_down = (
        lax.psum_scatter(
            jnp.stack(gate_up_terms).astype(jnp.bfloat16), "dp", scatter_dimension=1, tiled=True
        ).astype(jnp.float32),
        lax.psum_scatter(
            jnp.stack(down_terms).astype(jnp.bfloat16), "dp", scatter_dimension=2, tiled=True
        ).astype(jnp.float32),
    )
    mean_factor = 1.0 / lax.axis_size("dp")
    grad_gate_up = (summed_gate_up * mean_factor).astype(jnp.bfloat16)
    grad_down = (summed_down * mean_factor).astype(jnp.bfloat16)
    back_flat = returned_in.reshape(all_experts * capacity, dim_model)
    route_flat = returned_route.reshape(all_experts * capacity)
    route_rows = jnp.take(back_flat, position, axis=0).reshape(tok_rows, top_count, dim_model)
    d_tokens = jnp.sum(route_rows.astype(jnp.float32), axis=1).astype(jnp.bfloat16)
    d_route = jnp.take(route_flat, position, axis=0).reshape(tok_rows, top_count)
    return (d_tokens, d_route, grad_gate_up, grad_down)


def solution(mesh):
    placed = (
        P(("expert", "dp"), None),
        P(("expert", "dp"), None),
        P(("expert", "dp"), None),
        P(("expert", "dp"), None),
        P("expert", None, None),
        P("expert", None, None),
    )
    return jax.shard_map(
        local,
        mesh=mesh,
        in_specs=placed,
        out_specs=(
            P(("expert", "dp"), None),
            P(("expert", "dp"), None),
            P("expert", "dp", None),
            P("expert", None, "dp"),
        ),
        check_vma=False,
    )
```

profile of v0, /device:TPU:0, one launch (start us, length us, event | category | flops | bytes accessed | tf_op | source)
XLA Modules:
  0.0 364.6 jit_solution(9369899892041569120)
XLA Ops:
  7.2 0.8 copy.32
  8.7 4.3 %scatter_custom_fusion = s32[1152]{0:T(1024)S(1)} fusion(s32[1024]{0:T(1024)S(1)} %bitcast.83, s32[1024]{0:T(1024)S(1)} %iota.30, s32[]{:T(128)} %constant.102.clone.1), kind=kCustom, calls=%fused_computation.119 | custom fusion | bytes 4612 | tf_op jit(solution)/shard_map/scatter | solution.py:90
  13.0 0.8 copy.38
  13.9 7.3 %gather_fusion = bf16[1152]{0:T(1024)(128)(2,1)S(1)} fusion(bf16[1024]{0:T(1024)(128)(2,1)S(1)} %reshape.244, s32[2048]{0:T(1024)S(1)} %pad_clamp_fusion.1), kind=kCustom, calls=%fused_computation.2 | custom fusion | bytes 9216 | tf_op jit(solution)/shard_map/jit(_take)/gather | solution.py:98
  21.3 0.6 copy.39
  21.9 5.2 %all-to-all-start = ((bf16[2,8,72]{2,0,1:T(2,128)(2,1)}), bf16[2,8,72]{2,0,1:T(2,128)(2,1)S(1)}, u32[]{:S(2)}, u32[]{:S(2)}) async-start(bf16[2,8,72]{2,0,1:T(2,128)(2,1)} %copy.39), calls=%async_computation | async-start | bytes 8192 | tf_op jit(solution)/shard_map/all_to_all | solution.py:106
  27.2 5.9 %gather_fusion.3 = bf16[1152,2048]{1,0:T(8,128)(2,1)} fusion(bf16[128,2048]{1,0:T(8,128)(2,1)S(1)} %copy-done, s32[2048]{0:T(1024)S(1)} %pad_clamp_fusion), kind=kCustom, calls=%fused_computation.clone | custom fusion | bytes 9441792 | tf_op jit(solution)/shard_map/jit(_take)/gather | solution.py:95
  33.1 5.9 %gather_fusion.4 = bf16[1152,2048]{1,0:T(8,128)(2,1)} fusion(bf16[128,2048]{1,0:T(8,128)(2,1)S(1)} %copy-done.2, s32[2048]{0:T(1024)S(1)} %pad_clamp_fusion), kind=kCustom, calls=%fused_computation.1.clone | custom fusion | bytes 9441792 | tf_op jit(solution)/shard_map/jit(_take)/gather | solution.py:92
  39.0 5.7 %broadcast_select_fusion = (bf16[1152,2048]{1,0:T(8,128)(2,1)S(1)}, bf16[1152,2048]{1,0:T(8,128)(2,1)}) fusion(bf16[1152,2048]{1,0:T(8,128)(2,1)} %gather_fusion.4, pred[1152]{0:T(1024)(128)(4,1)S(1)} %get-tuple-element.25, bf16[1152,2048]{1,0:T(8,128)(2,1)} %gather_fusion.3), kind=kLoop, calls=%fused_computation.8 | loop fusion | flops 4718592 | bytes 18875520 | tf_op jit(solution)/shard_map/jit(_take)/select_n | solution.py:92
  44.7 2.6 copy.41
  47.3 4.6 %all-to-all-start.2 = ((bf16[2,8,72,2048]{3,2,0,1:T(8,128)(2,1)}), bf16[2,8,72,2048]{3,2,0,1:T(8,128)(2,1)}, u32[]{:S(2)}, u32[]{:S(2)}) async-start(bf16[2,8,72,2048]{3,2,0,1:T(8,128)(2,1)} %copy.41), calls=%async_computation.2 | async-start | bytes 9437184 | tf_op jit(solution)/shard_map/all_to_all | solution.py:104
  51.9 5.2 %copy.40 = bf16[2,8,72,2048]{3,2,0,1:T(8,128)(2,1)} copy(bf16[2,8,72,2048]{3,2,1,0:T(8,128)(2,1)} %bitcast.70) | data formatting | bytes 9437184 | tf_op jit(solution)/shard_map/reshape | solution.py:95
  57.1 49.6 %all-to-all-done.2 = bf16[2,8,72,2048]{3,2,0,1:T(8,128)(2,1)} async-done(((bf16[2,8,72,2048]{3,2,0,1:T(8,128)(2,1)}), bf16[2,8,72,2048]{3,2,0,1:T(8,128)(2,1)}, u32[]{:S(2)}, u32[]{:S(2)}) %all-to-all-start.2) | async-done | bytes 4718624 | tf_op jit(solution)/shard_map/all_to_all | solution.py:104
  106.6 4.6 %all-to-all-start.1 = ((bf16[2,8,72,2048]{3,2,0,1:T(8,128)(2,1)}), bf16[2,8,72,2048]{3,2,0,1:T(8,128)(2,1)}, u32[]{:S(2)}, u32[]{:S(2)}) async-start(bf16[2,8,72,2048]{3,2,0,1:T(8,128)(2,1)} %copy.40), calls=%async_computation.1 | async-start | bytes 9437184 | tf_op jit(solution)/shard_map/all_to_all | solution.py:105
  111.2 0.2 reduce-scatter.5.cloned.1.call-start
  111.7 2.8 fusion.68
  114.4 1.4 copy-done.3
  115.8 5.2 %fusion.7 = f32[576,768]{1,0:T(8,128)} fusion(bf16[576,2048]{1,0:T(8,128)(2,1)S(1)} %bitcast.78, bf16[2,2048,768]{2,1,0:T(8,128)(2,1)} %param.12), kind=kOutput, calls=%fused_computation.21 | convolution fusion | flops 1811939328 | bytes 7274496 | tf_op jit(solution)/shard_map/dot_general | solution.py:8
  121.0 45.0 %all-to-all-done.1 = bf16[2,8,72,2048]{3,2,0,1:T(8,128)(2,1)} async-done(((bf16[2,8,72,2048]{3,2,0,1:T(8,128)(2,1)}), bf16[2,8,72,2048]{3,2,0,1:T(8,128)(2,1)}, u32[]{:S(2)}, u32[]{:S(2)}) %all-to-all-start.1) | async-done | bytes 4718624 | tf_op jit(solution)/shard_map/all_to_all | solution.py:105
  166.0 2.9 fusion.69
  168.9 0.4 copy-done.4
  169.3 0.5 copy-done.5
  169.8 2.5 fusion.32
  172.3 1.5 fusion.21
  173.9 2.0 fusion.3
  175.9 2.7 fusion.34
  178.6 1.5 fusion.22
  180.1 1.9 pad_maximum_fusion.2
  182.1 0.3 reduce-scatter.3.cloned.1.call-start
  182.3 0.7 copy-done.6
  183.1 4.4 %fusion.15 = bf16[1,2048,768]{2,1,0:T(8,128)(2,1)S(1)} fusion(bf16[576,2048]{1,0:T(8,128)(2,1)} %bitcast.79, bf16[576,384]{1,0:T(8,128)(2,1)S(1)} %get-tuple-element.35, bf16[576,384]{1,0:T(8,128)(2,1)S(1)} %copy-done.6), kind=kOutput, calls=%fused_computation.26 | convolution fusion | flops 1815281664 | bytes 6389760 | tf_op jit(solution)/shard_map/dot_general | solution.py:32
  187.5 2.9 fusion.16
  190.4 3.2 pad_maximum_fusion
  193.8 0.6 copy.45
  194.4 3.2 all-to-all-start.4
  197.7 4.2 %fusion.9 = bf16[576,2048]{1,0:T(8,128)(2,1)S(1)} fusion(bf16[2,2048,768]{2,1,0:T(8,128)(2,1)} %param.12, bf16[576,384]{1,0:T(8,128)(2,1)S(1)} %get-tuple-element.35, bf16[576,384]{1,0:T(8,128)(2,1)} %get-tuple-element.36), kind=kOutput, calls=%fused_computation.24 | convolution fusion | flops 1814888448 | bytes 6389760 | tf_op jit(solution)/shard_map/dot_general | solution.py:24
  202.0 2.0 fusion.12
  204.1 2.6 pad_maximum_fusion.1
  206.7 4.9 %all-to-all-start.3 = ((bf16[2,8,72,2048]{3,2,0,1:T(8,128)(2,1)}), bf16[2,8,72,2048]{3,2,0,1:T(8,128)(2,1)}, u32[]{:S(2)}, u32[]{:S(2)}) async-start(bf16[2,8,72,2048]{3,2,0,1:T(8,128)(2,1)} %pad_maximum_fusion.1), calls=%async_computation.3 | async-start | bytes 9437184 | tf_op jit(solution)/shard_map/all_to_all | solution.py:123
  211.8 6.8 %gather_fusion.2 = bf16[1024]{0:T(1024)(128)(2,1)S(1)} fusion(bf16[1152]{0:T(1024)(128)(2,1)S(1)} %reshape.248, s32[1024]{0:T(1024)S(1)} %broadcast_clamp_fusion), kind=kCustom, calls=%fused_computation.4 | custom fusion | bytes 8192 | tf_op jit(solution)/shard_map/jit(_take)/gather | solution.py:145
  218.8 0.7 copy.47
  219.5 46.8 %all-to-all-done.3 = bf16[2,8,72,2048]{3,2,0,1:T(8,128)(2,1)} async-done(((bf16[2,8,72,2048]{3,2,0,1:T(8,128)(2,1)}), bf16[2,8,72,2048]{3,2,0,1:T(8,128)(2,1)}, u32[]{:S(2)}, u32[]{:S(2)}) %all-to-all-start.3) | async-done | bytes 4718624 | tf_op jit(solution)/shard_map/all_to_all | solution.py:123
  266.3 5.3 %copy.44 = bf16[2,8,72,2048]{3,2,1,0:T(8,128)(2,1)} copy(bf16[2,8,72,2048]{3,2,0,1:T(8,128)(2,1)} %all-to-all-done.3) | data formatting | bytes 9437184 | tf_op jit(solution)/shard_map/all_to_all | solution.py:123
  271.5 11.8 %gather_fusion.1 = bf16[1024,2048]{1,0:T(8,128)(2,1)} fusion(bf16[1152,2048]{1,0:T(8,128)(2,1)} %bitcast.69, s32[1024]{0:T(1024)S(1)} %broadcast_clamp_fusion), kind=kCustom, calls=%fused_computation.3 | custom fusion | bytes 8392704 | tf_op jit(solution)/shard_map/jit(_take)/gather | solution.py:143
  283.3 5.2 %fusion = bf16[128,2048]{1,0:T(8,128)(2,1)} fusion(bf16[1024,2048]{1,0:T(8,128)(2,1)} %gather_fusion.1, pred[128,8]{1,0:T(8,128)(4,1)S(1)} %get-tuple-element.20), kind=kLoop, calls=%fused_computation.11 | loop fusion | flops 3932160 | bytes 4719616 | tf_op jit(solution)/shard_map/reduce_sum | solution.py:144
  288.5 2.2 multiply_convert_fusion.1
  290.6 64.3 %reduce-scatter.3.cloned.1.call-done = bf16[2,512,768]{2,1,0:T(8,128)(2,1)} async-done(((bf16[2,2048,768]{2,1,0:T(8,128)(2,1)}), bf16[2,512,768]{2,1,0:T(8,128)(2,1)}) %reduce-scatter.3.cloned.1.call-update) | async-done | bytes 1572880 | tf_op jit(solution)/shard_map/reduce_scatter | solution.py:131
  355.0 2.8 multiply_convert_fusion
  (60 shorter events, 1.7 us)
Async XLA Ops:
  7.2 20.0 %copy-start = (bf16[128,2048]{1,0:T(8,128)(2,1)S(1)}, bf16[128,2048]{1,0:T(8,128)(2,1)}, u32[]{:S(2)}) copy-start(bf16[128,2048]{1,0:T(8,128)(2,1)} %param.9) | copy-start | bytes 1572868
  21.9 25.3 %all-to-all-start = ((bf16[2,8,72]{2,0,1:T(2,128)(2,1)}), bf16[2,8,72]{2,0,1:T(2,128)(2,1)S(1)}, u32[]{:S(2)}, u32[]{:S(2)}) async-start(bf16[2,8,72]{2,0,1:T(2,128)(2,1)} %copy.39), calls=%async_computation | async-start | bytes 8192 | tf_op jit(solution)/shard_map/all_to_all | solution.py:106
  27.2 5.9 %copy-start.2 = (bf16[128,2048]{1,0:T(8,128)(2,1)S(1)}, bf16[128,2048]{1,0:T(8,128)(2,1)}, u32[]{:S(2)}) copy-start(bf16[128,2048]{1,0:T(8,128)(2,1)} %param.8) | copy-start | bytes 1572868
  47.3 59.4 %all-to-all-start.2 = ((bf16[2,8,72,2048]{3,2,0,1:T(8,128)(2,1)}), bf16[2,8,72,2048]{3,2,0,1:T(8,128)(2,1)}, u32[]{:S(2)}, u32[]{:S(2)}) async-start(bf16[2,8,72,2048]{3,2,0,1:T(8,128)(2,1)} %copy.41), calls=%async_computation.2 | async-start | bytes 9437184 | tf_op jit(solution)/shard_map/all_to_all | solution.py:104
  106.6 59.4 %all-to-all-start.1 = ((bf16[2,8,72,2048]{3,2,0,1:T(8,128)(2,1)}), bf16[2,8,72,2048]{3,2,0,1:T(8,128)(2,1)}, u32[]{:S(2)}, u32[]{:S(2)}) async-start(bf16[2,8,72,2048]{3,2,0,1:T(8,128)(2,1)} %copy.40), calls=%async_computation.1 | async-start | bytes 9437184 | tf_op jit(solution)/shard_map/all_to_all | solution.py:105
  111.2 177.3 %reduce-scatter.5.cloned.1.call-start = ((), (), s32[]{:S(2)}) async-start(), calls=%async_computation.8 | async-start | bytes 3932160 | tf_op jit(solution)/shard_map/reduce_scatter | solution.py:134
  114.4 1.4 copy-start.3
  166.0 3.3 copy-start.4
  166.0 3.8 %copy-start.5 = (f32[576,768]{1,0:T(8,128)S(1)}, f32[576,768]{1,0:T(8,128)}, u32[]{:S(2)}) copy-start(f32[576,768]{1,0:T(8,128)} %fusion.7) | copy-start | bytes 5308420
  166.0 7.9 %slice-start = ((s8[6291456]{0:T(1024)(128)(4,1)}), s8[4194304]{0:T(1024)(128)(4,1)S(1)}, s32[]{:S(2)}) async-start(s8[6291456]{0:T(1024)(128)(4,1)} %bitcast.85), calls=%async_computation.9 | async-start | bytes 8388608
  169.8 4.0 %slice-start.1 = ((s8[6291456]{0:T(1024)(128)(4,1)}), s8[2097152]{0:T(1024)(128)(4,1)S(1)}, s32[]{:S(2)}) async-start(s8[6291456]{0:T(1024)(128)(4,1)} %bitcast.85), calls=%async_computation.10 | async-start | bytes 4194304
  182.0 1.0 copy-start.6
  182.1 172.9 %reduce-scatter.3.cloned.1.call-start = ((), (), s32[]{:S(2)}) async-start(), calls=%async_computation.7 | async-start | bytes 7864320 | tf_op jit(solution)/shard_map/reduce_scatter | solution.py:131
  183.0 4.4 %copy-start.7 = (bf16[576,384]{1,0:T(8,128)(2,1)S(1)}, bf16[576,384]{1,0:T(8,128)(2,1)}, u32[]{:S(2)}) copy-start(bf16[576,384]{1,0:T(8,128)(2,1)} %get-tuple-element.37) | copy-start | bytes 1327108
  183.0 4.4 %copy-start.9 = (bf16[576,384]{1,0:T(8,128)(2,1)S(1)}, bf16[576,384]{1,0:T(8,128)(2,1)}, u32[]{:S(2)}) copy-start(bf16[576,384]{1,0:T(8,128)(2,1)} %get-tuple-element.38) | copy-start | bytes 1327108
  193.6 8.4 %slice-start.2 = ((s8[6291456]{0:T(1024)(128)(4,1)}), s8[2097152]{0:T(1024)(128)(4,1)S(1)}, s32[]{:S(2)}) async-start(s8[6291456]{0:T(1024)(128)(4,1)} %bitcast.87), calls=%async_computation.11 | async-start | bytes 4194304
  194.4 12.3 %all-to-all-start.4 = ((bf16[2,8,72]{2,0,1:T(2,128)(2,1)}), bf16[2,8,72]{2,0,1:T(2,128)(2,1)S(1)}, u32[]{:S(2)}, u32[]{:S(2)}) async-start(bf16[2,8,72]{2,0,1:T(2,128)(2,1)} %copy.45), calls=%async_computation.4 | async-start | bytes 8192 | tf_op jit(solution)/shard_map/all_to_all | solution.py:124
  197.7 4.3 %slice-start.3 = ((s8[6291456]{0:T(1024)(128)(4,1)}), s8[4194304]{0:T(1024)(128)(4,1)S(1)}, s32[]{:S(2)}) async-start(s8[6291456]{0:T(1024)(128)(4,1)} %bitcast.87), calls=%async_computation.12 | async-start | bytes 8388608
  197.7 4.3 %copy-start.8 = (bf16[576,384]{1,0:T(8,128)(2,1)S(1)}, bf16[576,384]{1,0:T(8,128)(2,1)}, u32[]{:S(2)}) copy-start(bf16[576,384]{1,0:T(8,128)(2,1)} %get-tuple-element.37) | copy-start | bytes 1327108
  197.7 4.3 %copy-start.10 = (bf16[576,384]{1,0:T(8,128)(2,1)S(1)}, bf16[576,384]{1,0:T(8,128)(2,1)}, u32[]{:S(2)}) copy-start(bf16[576,384]{1,0:T(8,128)(2,1)} %get-tuple-element.38) | copy-start | bytes 1327108
  206.7 59.6 %all-to-all-start.3 = ((bf16[2,8,72,2048]{3,2,0,1:T(8,128)(2,1)}), bf16[2,8,72,2048]{3,2,0,1:T(8,128)(2,1)}, u32[]{:S(2)}, u32[]{:S(2)}) async-start(bf16[2,8,72,2048]{3,2,0,1:T(8,128)(2,1)} %pad_maximum_fusion.1), calls=%async_computation.3 | async-start | bytes 9437184 | tf_op jit(solution)/shard_map/all_to_all | solution.py:123
  283.3 74.5 %copy-start.1 = (bf16[128,2048]{1,0:T(8,128)(2,1)S(1)}, bf16[128,2048]{1,0:T(8,128)(2,1)}, u32[]{:S(2)}) copy-start(bf16[128,2048]{1,0:T(8,128)(2,1)} %param.9) | copy-start | bytes 1572868
Sparse Core Ops, SparseCore 0:
  182.2 59.6 reduce-scatter.4
  244.2 110.7 reduce-scatter.2
where the time goes:
time: 365 us
  waiting for transfers between devices  206 us (56%)
  local copies, waits for them, and re-layouts  68.2 us (19%)
  matrix products  29.4 us (8%)
  other arithmetic  24 us (7%)
  starting transfers between devices  23 us (6%)
  between operations  14.4 us (4%)
    reduce_scatter x1, waiting for transfers between devices, local(): lax.psum_scatter(jnp.stack(gate_up_terms).astype(jnp.bfloat16), 'dp', sca...  64.3 us
    all_to_all x1, waiting for transfers between devices, local(): lax.all_to_all(send_in, 'expert', split_axis=1, concat_axis=1, tiled=True)  49.6 us
    all_to_all x1, waiting for transfers between devices, local(): lax.all_to_all(jnp.stack(inputs_list), 'expert', split_axis=1, concat_axi...  46.8 us
    all_to_all x1, waiting for transfers between devices, local(): lax.all_to_all(send_grad, 'expert', split_axis=1, concat_axis=1, tiled=True)  45 us
    gather x1, local copies, waits for them, and re-layouts, local(): jnp.take(back_flat, position, axis=0)  11.8 us
    dot_general x2, matrix products, weight_terms(): lax.dot_general(rows_in, grad_pre, (((0,), (0,)), ((), ())), preferred_el...  7.37 us
  transfers between devices with their start and end apart: 7, of which 4 were waited for; matrix products, arithmetic and copies ran while one was open for 24% of the time, Pallas kernels for 0%

commit v1 on v0

--- a/solution.py
+++ b/solution.py
@@ -102,7 +102,12 @@
     down_terms = []
     arrived_in, arrived_grad, arrived_weight = (
         lax.all_to_all(send_in, "expert", split_axis=1, concat_axis=1, tiled=True),
-        lax.all_to_all(send_grad, "expert", split_axis=1, concat_axis=1, tiled=True),
+        jnp.concatenate(
+            lax.all_to_all(
+                jnp.stack(jnp.split(send_grad, lax.axis_size("expert"), axis=1)), "expert", 0, 0
+            ),
+            axis=1,
+        ),
         lax.all_to_all(send_weight, "expert", split_axis=1, concat_axis=1, tiled=True),
     )
     inputs_list = []

time: 365 us -> 374 us (1.025)
  waiting for transfers between devices: 206 us -> 211 us
  local copies, waits for them, and re-layouts: 68.2 us -> 72.6 us
    reshape x1 -> x0, local copies, waits for them, and re-layouts: 5.18 us -> none  [local(): jnp.take(out_grad, token_of, axis=0, mode='fill', fill_value=0)]
    all_to_all x1, waiting for transfers between devices: 45 us -> 49.5 us  [local(): lax.all_to_all(jnp.stack(jnp.split(send_grad, lax.axis_size('expert'), ax...]
    unnamed x33 -> x46, local copies, waits for them, and re-layouts: 5.39 us -> 9.93 us
  transfers between devices with their start and end apart: 7 -> 7, of which waited for: 4 -> 4; matrix products, arithmetic and copies ran while one was open for 24% -> 23% of each run, Pallas kernels for 0% -> 0%
where the time goes in v1:
time: 374 us
  waiting for transfers between devices  211 us (56%)
  local copies, waits for them, and re-layouts  72.6 us (19%)
  matrix products  28.2 us (8%)
  other arithmetic  24 us (6%)
  starting transfers between devices  23 us (6%)
  between operations  14.5 us (4%)
    reduce_scatter x1, waiting for transfers between devices, local(): lax.psum_scatter(jnp.stack(gate_up_terms).astype(jnp.bfloat16), 'dp', sca...  65.1 us
    all_to_all x1, waiting for transfers between devices, local(): lax.all_to_all(send_in, 'expert', split_axis=1, concat_axis=1, tiled=True)  50 us
    all_to_all x1, waiting for transfers between devices, local(): lax.all_to_all(jnp.stack(jnp.split(send_grad, lax.axis_size('expert'), ax...  49.5 us
    all_to_all x1, waiting for transfers between devices, local(): lax.all_to_all(jnp.stack(inputs_list), 'expert', split_axis=1, concat_axi...  46.8 us
    gather x1, local copies, waits for them, and re-layouts, local(): jnp.take(back_flat, position, axis=0)  11.8 us
    unnamed x46, local copies, waits for them, and re-layouts  9.93 us
    dot_general x2, matrix products, expert_backward(): pre_act = jnp.dot(rows_in, gate_up, preferred_element_type=jnp.float32)  7.63 us
  transfers between devices with their start and end apart: 7, of which 4 were waited for; matrix products, arithmetic and copies ran while one was open for 23% of the time, Pallas kernels for 0%

profile of v1, /device:TPU:0, one launch (start us, length us, event | category | flops | bytes accessed | tf_op | source)
XLA Modules:
  0.0 373.7 jit_solution(11588539590754484071)
XLA Ops:
  7.2 0.8 copy.52
  8.7 4.3 %scatter_custom_fusion = s32[1152]{0:T(1024)S(1)} fusion(s32[1024]{0:T(1024)S(1)} %bitcast.137, s32[1024]{0:T(1024)S(1)} %iota.30, s32[]{:T(128)} %constant.102.clone.1), kind=kCustom, calls=%fused_computation.135 | custom fusion | bytes 4612 | tf_op jit(solution)/shard_map/scatter | solution.py:90
  13.0 0.8 copy.58
  14.0 7.3 %gather_fusion = bf16[1152]{0:T(1024)(128)(2,1)S(1)} fusion(bf16[1024]{0:T(1024)(128)(2,1)S(1)} %reshape.252, s32[2048]{0:T(1024)S(1)} %get-tuple-element.42), kind=kCustom, calls=%fused_computation.2 | custom fusion | bytes 9216 | tf_op jit(solution)/shard_map/jit(_take)/gather | solution.py:98
  22.0 5.2 %all-to-all-start = ((bf16[2,8,72]{2,0,1:T(2,128)(2,1)}), bf16[2,8,72]{2,0,1:T(2,128)(2,1)S(1)}, u32[]{:S(2)}, u32[]{:S(2)}) async-start(bf16[2,8,72]{2,0,1:T(2,128)(2,1)} %copy.59), calls=%async_computation | async-start | bytes 8192 | tf_op jit(solution)/shard_map/all_to_all | solution.py:111
  27.1 5.9 %gather_fusion.3 = bf16[1152,2048]{1,0:T(8,128)(2,1)} fusion(bf16[128,2048]{1,0:T(8,128)(2,1)S(1)} %copy-done, s32[2048]{0:T(1024)S(1)} %get-tuple-element.41), kind=kCustom, calls=%fused_computation.clone | custom fusion | bytes 9441792 | tf_op jit(solution)/shard_map/jit(_take)/gather | solution.py:95
  33.1 5.9 %gather_fusion.4 = bf16[1152,2048]{1,0:T(8,128)(2,1)} fusion(bf16[128,2048]{1,0:T(8,128)(2,1)S(1)} %copy-done.2, s32[2048]{0:T(1024)S(1)} %get-tuple-element.41), kind=kCustom, calls=%fused_computation.1.clone | custom fusion | bytes 9441792 | tf_op jit(solution)/shard_map/jit(_take)/gather | solution.py:92
  39.0 5.7 %broadcast_select_fusion = (bf16[1152,2048]{1,0:T(8,128)(2,1)}, bf16[1152,2048]{1,0:T(8,128)(2,1)S(1)}) fusion(bf16[1152,2048]{1,0:T(8,128)(2,1)} %gather_fusion.4, pred[1152]{0:T(1024)(128)(4,1)S(1)} %get-tuple-element.25, bf16[1152,2048]{1,0:T(8,128)(2,1)} %gather_fusion.3), kind=kLoop, calls=%fused_computation.8 | loop fusion | flops 4718592 | bytes 18875520 | tf_op jit(solution)/shard_map/jit(_take)/select_n | solution.py:92
  44.7 0.9 fusion.45
  45.6 0.9 fusion.44
  46.5 0.9 fusion.43
  47.4 0.9 fusion.42
  48.2 0.9 fusion.41
  49.1 0.9 fusion.40
  50.0 0.9 fusion.39
  50.8 0.9 fusion.38
  51.7 4.6 %all-to-all-start.1 = ((bf16[8,2,1,72,2048]{4,3,1,2,0:T(8,128)(2,1)}), bf16[8,2,1,72,2048]{4,3,1,2,0:T(8,128)(2,1)}, u32[]{:S(2)}, u32[]{:S(2)}) async-start(bf16[8,2,1,72,2048]{4,3,1,2,0:T(8,128)(2,1)} %fusion.38), calls=%async_computation.1 | async-start | bytes 9437184 | tf_op jit(solution)/shard_map/all_to_all | solution.py:106
  56.4 5.2 %copy.67 = bf16[2,8,72,2048]{3,2,0,1:T(8,128)(2,1)} copy(bf16[2,8,72,2048]{3,2,1,0:T(8,128)(2,1)} %bitcast.117) | data formatting | bytes 9437184 | tf_op jit(solution)/shard_map/reshape | solution.py:92
  61.6 49.5 %all-to-all-done.1 = bf16[8,2,1,72,2048]{4,3,1,2,0:T(8,128)(2,1)} async-done(((bf16[8,2,1,72,2048]{4,3,1,2,0:T(8,128)(2,1)}), bf16[8,2,1,72,2048]{4,3,1,2,0:T(8,128)(2,1)}, u32[]{:S(2)}, u32[]{:S(2)}) %all-to-all-start.1) | async-done | bytes 4718624 | tf_op jit(solution)/shard_map/all_to_all | solution.py:106
  111.1 4.6 %all-to-all-start.2 = ((bf16[2,8,72,2048]{3,2,0,1:T(8,128)(2,1)}), bf16[2,8,72,2048]{3,2,0,1:T(8,128)(2,1)}, u32[]{:S(2)}, u32[]{:S(2)}) async-start(bf16[2,8,72,2048]{3,2,0,1:T(8,128)(2,1)} %copy.67), calls=%async_computation.2 | async-start | bytes 9437184 | tf_op jit(solution)/shard_map/all_to_all | solution.py:104
  116.1 4.3 %fusion.77 = (bf16[1,8,1,72,2048]{4,3,0,2,1:T(8,128)(2,1)}, bf16[1,8,1,72,2048]{4,3,0,2,1:T(8,128)(2,1)S(1)}) fusion(bf16[2,8,1,72,2048]{4,3,0,2,1:T(8,128)(2,1)} %bitcast.13), kind=kLoop, calls=%fused_computation.145 | loop fusion | bytes 9437184 | tf_op jit(solution)/shard_map/slice | solution.py:119
  120.5 50.0 %all-to-all-done.2 = bf16[2,8,72,2048]{3,2,0,1:T(8,128)(2,1)} async-done(((bf16[2,8,72,2048]{3,2,0,1:T(8,128)(2,1)}), bf16[2,8,72,2048]{3,2,0,1:T(8,128)(2,1)}, u32[]{:S(2)}, u32[]{:S(2)}) %all-to-all-start.2) | async-done | bytes 4718624 | tf_op jit(solution)/shard_map/all_to_all | solution.py:104
  170.5 2.8 fusion.76
  173.3 5.6 %fusion.7 = f32[576,768]{1,0:T(8,128)S(1)} fusion(bf16[576,2048]{1,0:T(8,128)(2,1)S(1)} %bitcast.132, bf16[2,2048,768]{2,1,0:T(8,128)(2,1)} %param.12), kind=kOutput, calls=%fused_computation.21 | convolution fusion | flops 1811939328 | bytes 7274496 | tf_op jit(solution)/shard_map/dot_general | solution.py:8
  178.9 2.5 fusion.32
  181.5 1.5 fusion.21
  183.0 2.0 fusion.3
  185.0 2.7 fusion.34
  187.7 1.5 fusion.22
  189.2 1.9 pad_maximum_fusion.2
  191.4 1.4 copy-done.7
  192.9 2.9 fusion.15
  195.8 2.9 fusion.16
  198.7 3.2 pad_maximum_fusion
  202.7 3.3 all-to-all-start.4
  206.0 4.2 %fusion.9 = bf16[576,2048]{1,0:T(8,128)(2,1)S(1)} fusion(bf16[2,2048,768]{2,1,0:T(8,128)(2,1)} %param.12, bf16[576,384]{1,0:T(8,128)(2,1)S(1)} %get-tuple-element.35, bf16[576,384]{1,0:T(8,128)(2,1)} %get-tuple-element.36), kind=kOutput, calls=%fused_computation.24 | convolution fusion | flops 1814888448 | bytes 6389760 | tf_op jit(solution)/shard_map/dot_general | solution.py:24
  210.3 2.0 fusion.12
  212.4 2.6 pad_maximum_fusion.1
  215.0 4.9 %all-to-all-start.3 = ((bf16[2,8,72,2048]{3,2,0,1:T(8,128)(2,1)}), bf16[2,8,72,2048]{3,2,0,1:T(8,128)(2,1)}, u32[]{:S(2)}, u32[]{:S(2)}) async-start(bf16[2,8,72,2048]{3,2,0,1:T(8,128)(2,1)} %pad_maximum_fusion.1), calls=%async_computation.3 | async-start | bytes 9437184 | tf_op jit(solution)/shard_map/all_to_all | solution.py:128
  220.1 6.8 %gather_fusion.2 = bf16[1024]{0:T(1024)(128)(2,1)S(1)} fusion(bf16[1152]{0:T(1024)(128)(2,1)S(1)} %reshape.257, s32[1024]{0:T(1024)S(1)} %broadcast_clamp_fusion), kind=kCustom, calls=%fused_computation.4 | custom fusion | bytes 8192 | tf_op jit(solution)/shard_map/jit(_take)/gather | solution.py:150
  227.1 0.7 copy.73
  227.7 46.8 %all-to-all-done.3 = bf16[2,8,72,2048]{3,2,0,1:T(8,128)(2,1)} async-done(((bf16[2,8,72,2048]{3,2,0,1:T(8,128)(2,1)}), bf16[2,8,72,2048]{3,2,0,1:T(8,128)(2,1)}, u32[]{:S(2)}, u32[]{:S(2)}) %all-to-all-start.3) | async-done | bytes 4718624 | tf_op jit(solution)/shard_map/all_to_all | solution.py:128
  274.6 5.3 %copy.70 = bf16[2,8,72,2048]{3,2,1,0:T(8,128)(2,1)} copy(bf16[2,8,72,2048]{3,2,0,1:T(8,128)(2,1)} %all-to-all-done.3) | data formatting | bytes 9437184 | tf_op jit(solution)/shard_map/all_to_all | solution.py:128
  279.8 11.8 %gather_fusion.1 = bf16[1024,2048]{1,0:T(8,128)(2,1)} fusion(bf16[1152,2048]{1,0:T(8,128)(2,1)} %bitcast.116, s32[1024]{0:T(1024)S(1)} %broadcast_clamp_fusion), kind=kCustom, calls=%fused_computation.3 | custom fusion | bytes 8392704 | tf_op jit(solution)/shard_map/jit(_take)/gather | solution.py:148
  291.6 5.2 %fusion = bf16[128,2048]{1,0:T(8,128)(2,1)} fusion(bf16[1024,2048]{1,0:T(8,128)(2,1)} %gather_fusion.1, pred[128,8]{1,0:T(8,128)(4,1)S(1)} %get-tuple-element.20), kind=kLoop, calls=%fused_computation.11 | loop fusion | flops 3932160 | bytes 4719616 | tf_op jit(solution)/shard_map/reduce_sum | solution.py:149
  296.8 2.2 multiply_convert_fusion.1
  299.0 65.1 %reduce-scatter.3.cloned.1.call-done = bf16[2,512,768]{2,1,0:T(8,128)(2,1)} async-done(((bf16[2,2048,768]{2,1,0:T(8,128)(2,1)}), bf16[2,512,768]{2,1,0:T(8,128)(2,1)}) %reduce-scatter.3.cloned.1.call-update) | async-done | bytes 1572880 | tf_op jit(solution)/shard_map/reduce_scatter | solution.py:136
  364.1 2.8 multiply_convert_fusion
  (72 shorter events, 3.5 us)
Async XLA Ops:
  7.2 20.0 %copy-start = (bf16[128,2048]{1,0:T(8,128)(2,1)S(1)}, bf16[128,2048]{1,0:T(8,128)(2,1)}, u32[]{:S(2)}) copy-start(bf16[128,2048]{1,0:T(8,128)(2,1)} %param.9) | copy-start | bytes 1572868
  22.0 29.8 %all-to-all-start = ((bf16[2,8,72]{2,0,1:T(2,128)(2,1)}), bf16[2,8,72]{2,0,1:T(2,128)(2,1)S(1)}, u32[]{:S(2)}, u32[]{:S(2)}) async-start(bf16[2,8,72]{2,0,1:T(2,128)(2,1)} %copy.59), calls=%async_computation | async-start | bytes 8192 | tf_op jit(solution)/shard_map/all_to_all | solution.py:111
  27.1 5.9 %copy-start.2 = (bf16[128,2048]{1,0:T(8,128)(2,1)S(1)}, bf16[128,2048]{1,0:T(8,128)(2,1)}, u32[]{:S(2)}) copy-start(bf16[128,2048]{1,0:T(8,128)(2,1)} %param.8) | copy-start | bytes 1572868
  51.7 59.4 %all-to-all-start.1 = ((bf16[8,2,1,72,2048]{4,3,1,2,0:T(8,128)(2,1)}), bf16[8,2,1,72,2048]{4,3,1,2,0:T(8,128)(2,1)}, u32[]{:S(2)}, u32[]{:S(2)}) async-start(bf16[8,2,1,72,2048]{4,3,1,2,0:T(8,128)(2,1)} %fusion.38), calls=%async_computation.1 | async-start | bytes 9437184 | tf_op jit(solution)/shard_map/all_to_all | solution.py:106
  111.1 59.4 %all-to-all-start.2 = ((bf16[2,8,72,2048]{3,2,0,1:T(8,128)(2,1)}), bf16[2,8,72,2048]{3,2,0,1:T(8,128)(2,1)}, u32[]{:S(2)}, u32[]{:S(2)}) async-start(bf16[2,8,72,2048]{3,2,0,1:T(8,128)(2,1)} %copy.67), calls=%async_computation.2 | async-start | bytes 9437184 | tf_op jit(solution)/shard_map/all_to_all | solution.py:104
  115.7 181.1 %reduce-scatter.5.cloned.1.call-start = ((), (), s32[]{:S(2)}) async-start(), calls=%async_computation.8 | async-start | bytes 3932160 | tf_op jit(solution)/shard_map/reduce_scatter | solution.py:139
  173.2 5.7 %copy-start.6 = (bf16[1,8,72,2048]{3,2,0,1:T(8,128)(2,1)}, bf16[1,8,72,2048]{3,2,0,1:T(8,128)(2,1)S(1)}, u32[]{:S(2)}) copy-start(bf16[1,8,72,2048]{3,2,0,1:T(8,128)(2,1)S(1)} %get-tuple-element.27) | copy-start | bytes 7077892
  173.2 9.8 %copy-start.4 = (bf16[1,8,72,2048]{3,2,0,1:T(8,128)(2,1)}, bf16[1,8,72,2048]{3,2,0,1:T(8,128)(2,1)S(1)}, u32[]{:S(2)}) copy-start(bf16[1,8,72,2048]{3,2,0,1:T(8,128)(2,1)S(1)} %get-tuple-element.28) | copy-start | bytes 7077892
  173.2 5.7 %copy-start.3 = (bf16[1,8,1,72,2048]{4,3,0,2,1:T(8,128)(2,1)S(1)}, bf16[1,8,1,72,2048]{4,3,0,2,1:T(8,128)(2,1)}, u32[]{:S(2)}) copy-start(bf16[1,8,1,72,2048]{4,3,0,2,1:T(8,128)(2,1)} %get-tuple-element.29) | copy-start | bytes 7077892
  173.2 5.7 %copy-start.8 = (bf16[2,384,2048]{2,1,0:T(8,128)(2,1)S(1)}, bf16[2,384,2048]{2,1,0:T(8,128)(2,1)}, u32[]{:S(2)}) copy-start(bf16[2,384,2048]{2,1,0:T(8,128)(2,1)} %param.13) | copy-start | bytes 9437188
  173.2 9.7 %slice-start = ((s8[6291456]{0:T(1024)(128)(4,1)}), s8[2097152]{0:T(1024)(128)(4,1)S(1)}, s32[]{:S(2)}) async-start(s8[6291456]{0:T(1024)(128)(4,1)} %bitcast.139), calls=%async_computation.9 | async-start | bytes 4194304
  178.9 4.1 %slice-start.1 = ((s8[6291456]{0:T(1024)(128)(4,1)}), s8[4194304]{0:T(1024)(128)(4,1)S(1)}, s32[]{:S(2)}) async-start(s8[6291456]{0:T(1024)(128)(4,1)} %bitcast.139), calls=%async_computation.10 | async-start | bytes 8388608
  191.1 1.7 copy-start.7
  191.1 1.7 copy-start.9
  191.2 172.9 %reduce-scatter.3.cloned.1.call-start = ((), (), s32[]{:S(2)}) async-start(), calls=%async_computation.7 | async-start | bytes 7864320 | tf_op jit(solution)/shard_map/reduce_scatter | solution.py:136
  192.9 2.9 copy-start.5
  192.9 2.9 copy-start.10
  192.9 2.9 copy-start.12
  201.9 8.3 %slice-start.2 = ((s8[6291456]{0:T(1024)(128)(4,1)}), s8[2097152]{0:T(1024)(128)(4,1)S(1)}, s32[]{:S(2)}) async-start(s8[6291456]{0:T(1024)(128)(4,1)} %bitcast.141), calls=%async_computation.11 | async-start | bytes 4194304
  202.7 12.3 %all-to-all-start.4 = ((bf16[2,8,72]{2,0,1:T(2,128)(2,1)}), bf16[2,8,72]{2,0,1:T(2,128)(2,1)S(1)}, u32[]{:S(2)}, u32[]{:S(2)}) async-start(bf16[2,8,72]{2,0,1:T(2,128)(2,1)} %copy.71), calls=%async_computation.4 | async-start | bytes 8192 | tf_op jit(solution)/shard_map/all_to_all | solution.py:129
  206.0 4.3 %slice-start.3 = ((s8[6291456]{0:T(1024)(128)(4,1)}), s8[4194304]{0:T(1024)(128)(4,1)S(1)}, s32[]{:S(2)}) async-start(s8[6291456]{0:T(1024)(128)(4,1)} %bitcast.141), calls=%async_computation.12 | async-start | bytes 8388608
  206.0 4.3 %copy-start.11 = (bf16[576,384]{1,0:T(8,128)(2,1)S(1)}, bf16[576,384]{1,0:T(8,128)(2,1)}, u32[]{:S(2)}) copy-start(bf16[576,384]{1,0:T(8,128)(2,1)} %get-tuple-element.37) | copy-start | bytes 1327108
  206.0 4.3 %copy-start.13 = (bf16[576,384]{1,0:T(8,128)(2,1)S(1)}, bf16[576,384]{1,0:T(8,128)(2,1)}, u32[]{:S(2)}) copy-start(bf16[576,384]{1,0:T(8,128)(2,1)} %get-tuple-element.38) | copy-start | bytes 1327108
  215.0 59.6 %all-to-all-start.3 = ((bf16[2,8,72,2048]{3,2,0,1:T(8,128)(2,1)}), bf16[2,8,72,2048]{3,2,0,1:T(8,128)(2,1)}, u32[]{:S(2)}, u32[]{:S(2)}) async-start(bf16[2,8,72,2048]{3,2,0,1:T(8,128)(2,1)} %pad_maximum_fusion.1), calls=%async_computation.3 | async-start | bytes 9437184 | tf_op jit(solution)/shard_map/all_to_all | solution.py:128
  291.6 75.3 %copy-start.1 = (bf16[128,2048]{1,0:T(8,128)(2,1)S(1)}, bf16[128,2048]{1,0:T(8,128)(2,1)}, u32[]{:S(2)}) copy-start(bf16[128,2048]{1,0:T(8,128)(2,1)} %param.9) | copy-start | bytes 1572868
Sparse Core Ops, SparseCore 0:
  191.3 59.6 reduce-scatter.4
  253.3 110.7 reduce-scatter.2
